TPU v7x, 32 devices: a whole 2x2x4 slice. The times are simulated.
32 devices in a mesh: groups: 2 (over y), seq: 4 (over z), head: 2 (over x), sub: 2 (over core).
Axes of the slice: x: 2, y: 2, z: 4, core: 2. Of those that a mesh axis runs over, the one named last changes fastest.
Arguments:
- tokens: int32 [3, 4096], P(None, ('groups', 'seq')), parts along dimension 1, may hold values from 0 to 1023
- masked: int32 [4096], P(('groups', 'seq')), parts along dimension 0, may hold values 0 or 1
- used_frames: int32 [2], P('groups'), parts along dimension 0, may hold values from 1024 to 2048
- tables: bfloat16 [3, 1024, 1024], P(None, None, ('head', 'sub')), may hold values from -6 to 6
- mask_vec: bfloat16 [1024], P(('head', 'sub')), may hold values from -6 to 6
- attn_in: bfloat16 [3, 1024, 512], P(None, None, ('head', 'sub')), may hold values from -0.1875 to 0.1875
- head_temp: float32 [8], P(('head', 'sub')), may hold values from 12 to 28
- attn_out: bfloat16 [512, 1024], P(('head', 'sub')), may hold values from -0.25 to 0.25
- conv_in: bfloat16 [2, 1024, 1024], P(None, None, ('head', 'sub')), may hold values from -0.1875 to 0.1875
- conv_kernel: float32 [31, 1024], P(None, ('head', 'sub')), may hold values from -1 to 1
- conv_out: bfloat16 [1024, 1024], P(('head', 'sub')), may hold values from -0.1875 to 0.1875
- voc_in: bfloat16 [1024, 512], P(('head', 'sub')), may hold values from -0.1875 to 0.1875
- voc_kernel: float32 [7, 512], replicated, may hold values from -2 to 2
- voc_up: bfloat16 [512, 1536], P(('head', 'sub')), may hold values from -0.25 to 0.25
- voc_down: bfloat16 [1536, 512], P(('head', 'sub')), may hold values from -0.15625 to 0.15625
- voc_head: bfloat16 [512, 1282], P(('head', 'sub')), may hold values from -0.25 to 0.25
- head_bias: float32 [1282], replicated, may hold values from 0.5 to 2.5
Outputs:
- features: bfloat16 [4096, 1024], P(('groups', 'seq', 'head', 'sub')), parts along dimension 0
- waveform: float32 [1310720], P(('groups', 'seq', 'head', 'sub')), parts along dimension 0
There are 2 independent parts, one for each index of `groups`. A program takes and returns all parts, laid end to end along the dimension named above; an argument that names none is the same for every part. Nothing has to cross between parts.
All inputs are finite; a program needn't handle non-finite values. No bound on the sum of `masked` on one device may be relied on, other than what follows from the above.
Results may differ from a plain program's by a relative error of at most 0.02.
Values may be sent and summed in bfloat16 or wider, within the bound.
A program may use at most 64 MiB of HBM per device.

v0:
```python
import math
import jax
import jax.numpy as jnp
from jax import lax
from jax.sharding import PartitionSpec as P

HOP = 320


def with_halo(x, sides, width):
    for axis, dim in sides:
        size, length = (lax.axis_size(axis), x.shape[dim])
        up = [(i, (i + 1) % size) for i in range(size - 1)]
        down = [(j, i) for i, j in up]
        last = lax.slice_in_dim(x, length - width, length, axis=dim)
        initial = lax.slice_in_dim(x, 0, width, axis=dim)
        before = lax.ppermute(last, axis, up)
        after = lax.ppermute(initial, axis, down)
        x = jnp.concatenate([before, x, after], axis=dim)
    return x


def layer_norm(values):
    average = jnp.mean(values, axis=-1, keepdims=True)
    centered = values - average
    return centered * lax.rsqrt(jnp.mean(centered * centered, axis=-1, keepdims=True) + 1e-05)


def unit_heads(projected, head_count):
    row_count = projected.shape[0]
    split_heads = projected.reshape(row_count, head_count, projected.shape[1] // head_count)
    scaled = split_heads * lax.rsqrt(
        jnp.sum(split_heads * split_heads, axis=-1, keepdims=True) + 1e-06
    )
    return scaled.astype(jnp.bfloat16)


def depthwise(kernel, padded_rows):
    tap_count = kernel.shape[0]
    out_rows = padded_rows.shape[0] - tap_count + 1
    result = jnp.zeros((out_rows, padded_rows.shape[1]), jnp.float32)
    for offset in range(tap_count):
        result = result + kernel[offset] * padded_rows[offset : offset + out_rows].astype(
            jnp.float32
        )
    return result


def attend_block(
    paired_sums,
    key_tile_rows,
    value_tile_rows,
    leading_row,
    query_normalized,
    similarity_sharpness,
    frame_ceiling,
):
    weighted, normalizer = paired_sums
    row_count = key_tile_rows.shape[0]
    angular_similarity = jnp.einsum(
        "qhd,khd->hqk", query_normalized, key_tile_rows, preferred_element_type=jnp.float32
    )
    token_position = leading_row + lax.broadcasted_iota(jnp.int32, (1, 1, row_count), 2)
    attention_probabilities = jnp.where(
        token_position < frame_ceiling,
        jnp.exp(similarity_sharpness[:, None, None] * (angular_similarity - 1.0)),
        0.0,
    )
    normalizer = normalizer + jnp.sum(attention_probabilities, axis=2).T
    weighted = weighted + jnp.einsum(
        "hqk,khd->qhd",
        attention_probabilities.astype(jnp.bfloat16),
        value_tile_rows,
        preferred_element_type=jnp.float32,
    )
    return (weighted, normalizer)


def synthesis_tables(bin_count, fft_size):
    bin_ids = lax.broadcasted_iota(jnp.int32, (bin_count, fft_size), 0)
    sample_ids = lax.broadcasted_iota(jnp.int32, (bin_count, fft_size), 1)
    phase_angle = 2.0 * math.pi / fft_size * (bin_ids * sample_ids % fft_size).astype(jnp.float32)
    edge_bin = (bin_ids == 0) | (bin_ids == bin_count - 1)
    factor = jnp.where(edge_bin, 1.0, 2.0) / fft_size
    cos_table = factor * jnp.cos(phase_angle)
    sin_table = jnp.where(edge_bin, 0.0, -factor * jnp.sin(phase_angle))
    return jnp.concatenate([cos_table, sin_table], axis=0)


def local(
    tokens,
    masked,
    used_frames,
    tables,
    mask_vec,
    attn_in,
    head_temp,
    attn_out,
    conv_in,
    conv_kernel,
    conv_out,
    voc_in,
    voc_kernel,
    voc_up,
    voc_down,
    voc_head,
    head_bias,
):
    frame_count = tokens.shape[1]
    group_count = lax.axis_size(("head", "sub"))
    group_index = lax.axis_index(("head", "sub"))
    seq_index = lax.axis_index("seq")
    slab_rows = frame_count // group_count
    frame_ceiling = used_frames[0]
    total_frames = frame_count * lax.axis_size("seq")
    code_ids = lax.broadcasted_iota(jnp.int32, (frame_count, tables.shape[1]), 1)
    masked_rows = masked == 1
    embedded = masked_rows.astype(jnp.float32)[:, None] * mask_vec.astype(jnp.float32)[None, :]
    for rvq_level in range(3):
        matches = tokens[rvq_level][:, None] == code_ids
        if rvq_level == 2:
            matches = matches & jnp.logical_not(masked_rows)[:, None]
        embedded = embedded + jnp.dot(
            matches.astype(jnp.bfloat16), tables[rvq_level], preferred_element_type=jnp.float32
        )
    embedded = embedded.astype(jnp.bfloat16)
    inputs, voc_in_full, voc_up_full, voc_down_full, voc_head_full = (
        lax.all_gather(embedded, ("head", "sub"), axis=1, tiled=True),
        lax.all_gather(voc_in, ("head", "sub"), axis=0, tiled=True),
        lax.all_gather(voc_up, ("head", "sub"), axis=0, tiled=True),
        lax.all_gather(voc_down, ("head", "sub"), axis=0, tiled=True),
        lax.all_gather(voc_head, ("head", "sub"), axis=0, tiled=True),
    )
    normed = layer_norm(inputs.astype(jnp.float32)).astype(jnp.bfloat16)
    local_heads = head_temp.shape[0]
    query_normalized = unit_heads(
        jnp.dot(normed, attn_in[0], preferred_element_type=jnp.float32), local_heads
    )
    key_unit = unit_heads(
        jnp.dot(normed, attn_in[1], preferred_element_type=jnp.float32), local_heads
    ).reshape(frame_count, -1)
    value_rows = jnp.dot(normed, attn_in[2], preferred_element_type=jnp.float32).astype(
        jnp.bfloat16
    )
    head_size = value_rows.shape[1] // local_heads
    start_pair = (
        jnp.zeros((frame_count, local_heads, head_size), jnp.float32),
        jnp.zeros((frame_count, local_heads), jnp.float32),
    )
    paired_sums = start_pair
    key_piece = lax.all_gather(key_unit, "seq", axis=0, tiled=True)
    value_piece = lax.all_gather(value_rows, "seq", axis=0, tiled=True)
    row_count = key_piece.shape[0]
    key_heads = key_piece.reshape(row_count, local_heads, head_size)
    value_heads = value_piece.reshape(row_count, local_heads, head_size)
    block_count = row_count // 512

    def scan_step(inner_pair, block_item):
        key_tile_rows, value_tile_rows, block_index = block_item
        return (
            attend_block(
                inner_pair,
                key_tile_rows,
                value_tile_rows,
                block_index * 512,
                query_normalized,
                head_temp,
                frame_ceiling,
            ),
            None,
        )

    block_items = (
        key_heads.reshape(block_count, 512, local_heads, head_size),
        value_heads.reshape(block_count, 512, local_heads, head_size),
        jnp.arange(block_count, dtype=jnp.int32),
    )
    paired_sums, _unused = lax.scan(scan_step, paired_sums, block_items)
    weighted, normalizer = paired_sums
    attended = (weighted / normalizer[:, :, None]).reshape(frame_count, -1).astype(jnp.bfloat16)
    head_part = jnp.dot(attended, attn_out, preferred_element_type=jnp.float32)
    fft_size = 2 * (head_bias.shape[0] // 2 - 1)
    intersection = fft_size // HOP
    half_voc = voc_kernel.shape[0] // 2
    vocoder_rim = half_voc + intersection // 2
    conv_reach = conv_kernel.shape[0] // 2 + vocoder_rim
    window_rows = slab_rows + 2 * vocoder_rim
    stream = inputs.astype(jnp.float32) + lax.psum(
        head_part.astype(jnp.bfloat16), ("head", "sub")
    ).astype(jnp.float32)
    stream_rims = with_halo(stream.astype(jnp.bfloat16), (("seq", 0),), conv_reach).astype(
        stream.dtype
    )
    conv_normed = layer_norm(stream_rims).astype(jnp.bfloat16)
    residual_window = lax.dynamic_slice_in_dim(
        stream_rims, group_index * slab_rows + conv_reach - vocoder_rim, window_rows, 0
    )
    gate_value = jnp.dot(conv_normed, conv_in[0], preferred_element_type=jnp.float32)
    gate_signal = jnp.dot(conv_normed, conv_in[1], preferred_element_type=jnp.float32)
    gated_rows = (gate_value * jax.nn.sigmoid(gate_signal)).astype(jnp.bfloat16)
    depth_rows = depthwise(conv_kernel, gated_rows)
    activated = (depth_rows * jax.nn.sigmoid(depth_rows)).astype(jnp.bfloat16)
    windows = jnp.stack(
        [
            activated[member * slab_rows : member * slab_rows + window_rows]
            for member in range(group_count)
        ]
    )
    partial_out = jnp.einsum("gsc,cd->gsd", windows, conv_out, preferred_element_type=jnp.float32)
    conv_sum = lax.psum_scatter(
        partial_out.astype(jnp.bfloat16), ("head", "sub"), scatter_dimension=0, tiled=True
    ).astype(jnp.float32)[0]
    block_norm = layer_norm(residual_window + conv_sum).astype(jnp.bfloat16)
    feature_out = block_norm[vocoder_rim : vocoder_rim + slab_rows]
    first_frame = seq_index * frame_count + group_index * slab_rows - vocoder_rim
    frame_ids = first_frame + lax.broadcasted_iota(jnp.int32, (window_rows, 1), 0)
    live_rows = (frame_ids >= 0) & (frame_ids < frame_ceiling)
    base_rows = layer_norm(
        jnp.where(
            live_rows, jnp.dot(block_norm, voc_in_full, preferred_element_type=jnp.float32), 0.0
        )
    )
    vdepth = depthwise(voc_kernel, base_rows)
    voc_rows = vdepth.shape[0]
    inner_rows = layer_norm(vdepth).astype(jnp.bfloat16)
    hidden = jax.nn.gelu(
        jnp.dot(inner_rows, voc_up_full, preferred_element_type=jnp.float32), approximate=False
    ).astype(jnp.bfloat16)
    refined = base_rows[half_voc : half_voc + voc_rows] + jnp.dot(
        hidden, voc_down_full, preferred_element_type=jnp.float32
    )
    head_input = layer_norm(refined).astype(jnp.bfloat16)
    spectrum = jnp.dot(head_input, voc_head_full, preferred_element_type=jnp.float32) + head_bias
    bin_count = spectrum.shape[1] // 2
    magnitude = jnp.minimum(jnp.exp(spectrum[:, :bin_count]), 100.0)
    phase_rows = spectrum[:, bin_count:]
    coefficients = jnp.concatenate(
        [magnitude * jnp.cos(phase_rows), magnitude * jnp.sin(phase_rows)], axis=1
    )
    wave_rows = jnp.dot(
        coefficients, synthesis_tables(bin_count, fft_size), precision=lax.Precision.HIGHEST
    )
    sample_ids = lax.broadcasted_iota(jnp.int32, (fft_size,), 0).astype(jnp.float32)
    hann_window = 0.5 - 0.5 * jnp.cos(2.0 * math.pi / fft_size * sample_ids)
    wave_ids = first_frame + half_voc + lax.broadcasted_iota(jnp.int32, (voc_rows, 1), 0)
    exists = ((wave_ids >= 0) & (wave_ids < total_frames)).astype(jnp.float32)
    framed = (wave_rows * hann_window[None, :] * exists).reshape(voc_rows, intersection, HOP)
    env_rows = (exists * (hann_window * hann_window)[None, :]).reshape(voc_rows, intersection, HOP)
    audio_sum = jnp.zeros((slab_rows, HOP), jnp.float32)
    energy = jnp.zeros((slab_rows, HOP), jnp.float32)
    for quarter in range(intersection):
        begin = intersection - quarter
        audio_sum = audio_sum + framed[begin : begin + slab_rows, quarter]
        energy = energy + env_rows[begin : begin + slab_rows, quarter]
    waveform = (audio_sum / energy).reshape(slab_rows * HOP)
    return (feature_out, waveform)


def solution(mesh):
    in_specs = (
        P(None, ("groups", "seq")),
        P(("groups", "seq")),
        P("groups"),
        P(None, None, ("head", "sub")),
        P(("head", "sub")),
        P(None, None, ("head", "sub")),
        P(("head", "sub")),
        P(("head", "sub"), None),
        P(None, None, ("head", "sub")),
        P(None, ("head", "sub")),
        P(("head", "sub"), None),
        P(("head", "sub"), None),
        P(),
        P(("head", "sub"), None),
        P(("head", "sub"), None),
        P(("head", "sub"), None),
        P(),
    )
    out_specs = (P(("groups", "seq", "head", "sub"), None), P(("groups", "seq", "head", "sub")))
    return jax.shard_map(local, mesh=mesh, in_specs=in_specs, out_specs=out_specs, check_vma=False)
```

profile of v0, /device:TPU:0, one launch (start us, length us, event | category | flops | bytes accessed | tf_op | source)
XLA Modules:
  0.0 276.2 jit_solution(7080855097597714248)
XLA Ops:
  12.6 2.3 fusion.41
  16.1 18.6 %all-gather.6.cloned.1.call-done = bf16[512,1024]{1,0:T(8,128)(2,1)} async-done(((bf16[512,256]{1,0:T(8,128)(2,1)}), bf16[512,1024]{1,0:T(8,128)(2,1)}) %all-gather.6.cloned.1.call-update) | async-done | bytes 1048592 | tf_op jit(solution)/shard_map/all_gather | solution.py:128
  40.1 16.0 %all_gather.23 = bf16[2048,128]{0,1:T(8,128)(2,1)S(1)} all-gather(bf16[512,128]{0,1:T(8,128)(2,1)S(1)} %bitcast.157), channel_id=1, replica_groups=mesh['groups'=2,'seq'=4,'head'=2,'sub'=2] {'seq'}, dimensions={0}, use_global_device_ids=true | all-gather | bytes 655360 | tf_op jit(solution)/shard_map/all_gather | solution.py:151
  57.3 1.9 copy.28
  59.2 2.1 multiply_reduce_fusion.5
  61.4 16.1 %all_gather.22 = bf16[2048,128]{1,0:T(8,128)(2,1)S(1)} all-gather(bf16[512,128]{1,0:T(8,128)(2,1)S(1)} %convolution_convert_fusion.2), channel_id=1, replica_groups=mesh['groups'=2,'seq'=4,'head'=2,'sub'=2] {'seq'}, dimensions={0}, use_global_device_ids=true | all-gather | bytes 655360 | tf_op jit(solution)/shard_map/all_gather | solution.py:152
  79.6 15.6 %while.15 = (s32[]{:T(128)}, f32[512,2,64]{0,2,1:T(8,128)S(1)}, f32[512,2]{0,1:T(2,128)S(1)}, bf16[4,512,2,64]{1,3,2,0:T(8,128)(2,1)S(1)}, s32[4]{0:T(128)S(1)},...) while((s32[]{:T(128)}, f32[512,2,64]{0,2,1:T(8,128)S(1)}, ...), condition=%wide.region_6.7_spmd.clone, body=%wide.region_4.6_spmd.clone.sunk | while | flops 136972288 | bytes 3032748 | solution.py:178
  95.3 2.4 convolution_convert_fusion.1
  97.9 36.0 %all-reduce.2.cloned.1.call-done = bf16[512,1024]{1,0:T(8,128)(2,1)} async-done(((bf16[512,1024]{1,0:T(8,128)(2,1)}), bf16[512,1024]{1,0:T(8,128)(2,1)}) %all-reduce.2.cloned.1.call-update) | async-done | bytes 1048592 | tf_op jit(solution)/shard_map/psum | solution.py:188
  133.9 1.7 fusion.26
  135.6 3.4 %collective-permute-start = (bf16[20,1024]{1,0:T(8,128)(2,1)S(1)}, bf16[20,1024]{1,0:T(8,128)(2,1)S(1)}, u32[]{:S(2)}, u32[]{:S(2)}) collective-permute-start(bf16[20,1024]{1,0:T(8,128)(2,1)S(1)} %get-tuple-element.190), channel_id=1, source_target_pairs={{0,4},{4,8},{8,12},{1,5},{5,9},{9,13},{2,6},{6,10},{10,14},{3,7},{... | collective-permute-start | bytes 122888 | tf_op jit(solution)/shard_map/ppermute | solution.py:17
  140.8 4.3 %collective-permute-done.1 = bf16[20,1024]{1,0:T(8,128)(2,1)S(1)} collective-permute-done((bf16[20,1024]{1,0:T(8,128)(2,1)S(1)}, bf16[20,1024]{1,0:T(8,128)(2,1)S(1)}, u32[]{:S(2)}, u32[]{:S(2)}) %collective-permute-start.1) | collective-permute-done | bytes 40992 | tf_op jit(solution)/shard_map/ppermute | solution.py:18
  147.6 2.3 multiply_convert_fusion.2
  155.0 15.1 %multiply_select_fusion = (f32[641,1280]{1,0:T(8,128)}, f32[641,1280]{1,0:T(8,128)}) fusion(f32[641]{0:T(1024)S(1)} %fusion.133, pred[641]{0:T(1024)(128)(4,1)S(1)} %fusion.132, f32[641]{0:T(1024)S(1)} %select_multiply_fusion), kind=kLoop, calls=%fused_computation.20 | loop fusion | flops 9845760 | bytes 6569609 | tf_op jit(solution)/shard_map/jit(_where)/select_n | solution.py:86
  170.1 1.8 fusion.166
  171.9 4.9 %reduce-scatter.2.cloned.1.call-done = bf16[1,138,1024]{2,1,0:T(8,128)(2,1)} async-done(((bf16[4,138,1024]{2,1,0:T(8,128)(2,1)}), bf16[1,138,1024]{2,1,0:T(8,128)(2,1)}) %reduce-scatter.2.cloned.1.call-update) | async-done | bytes 282640 | tf_op jit(solution)/shard_map/reduce_scatter | solution.py:210
  180.9 14.1 %all-gather.8.cloned.1.call-done = bf16[1024,512]{1,0:T(8,128)(2,1)} async-done(((bf16[256,512]{1,0:T(8,128)(2,1)}), bf16[1024,512]{1,0:T(8,128)(2,1)}) %all-gather.8.cloned.1.call-update) | async-done | bytes 1048592 | tf_op jit(solution)/shard_map/all_gather | solution.py:129
  198.3 17.7 %all-gather.10.cloned.1.call-done = bf16[512,1536]{1,0:T(8,128)(2,1)} async-done(((bf16[128,1536]{1,0:T(8,128)(2,1)}), bf16[512,1536]{1,0:T(8,128)(2,1)}) %all-gather.10.cloned.1.call-update) | async-done | bytes 1572880 | tf_op jit(solution)/shard_map/all_gather | solution.py:130
  216.0 21.1 %all-gather.12.cloned.1.call-done = bf16[1536,512]{1,0:T(8,128)(2,1)} async-done(((bf16[384,512]{1,0:T(8,128)(2,1)}), bf16[1536,512]{1,0:T(8,128)(2,1)}) %all-gather.12.cloned.1.call-update) | async-done | bytes 1572880 | tf_op jit(solution)/shard_map/all_gather | solution.py:131
  237.1 4.3 %fusion.178 = (f32[132]{0:T(256)S(1)}, f32[132,512]{1,0:T(8,128)S(1)}) fusion(bf16[1536,512]{1,0:T(8,128)(2,1)} %all-gather.12.cloned.1.call-done, bf16[512,1536]{1,0:T(8,128)(2,1)} %all-gather.10.cloned.1.call-done, f32[132,512]{1,0:T(8,128)S(1)} %get-tuple-element.185, f32[132]{0:T(256)S(1)} %add_rsqrt_fusion.5, f32[132]{0:T(256)S(1)} %broadcast_multiply_fusion.4, ...), kind=kOutput, calls=%fused_computation.260 | convolution fusion | flops 428752768 | bytes 3958320 | tf_op jit(solution)/shard_map/dot_general | solution.py:229
  241.6 15.4 %all-gather.14.cloned.1.call-done = bf16[512,1282]{0,1:T(8,128)(2,1)} async-done(((bf16[128,1282]{0,1:T(8,128)(2,1)}), bf16[512,1282]{0,1:T(8,128)(2,1)}) %all-gather.14.cloned.1.call-update) | async-done | bytes 1312784 | tf_op jit(solution)/shard_map/all_gather | solution.py:132
  257.0 2.1 convolution_add_fusion
  259.2 1.9 cosine_multiply_fusion.1
  261.1 6.2 %fusion.19 = f32[132,1280]{1,0:T(8,128)S(1)} fusion(f32[641,1280]{1,0:T(8,128)S(1)} %copy-done.2, f32[641,1280]{1,0:T(8,128)} %get-tuple-element.254, f32[132,641]{1,0:T(8,128)S(1)} %get-tuple-element.199, f32[132,641]{1,0:T(8,128)S(1)} %get-tuple-element.198, f32[132]{0:T(256)S(1)} %and_convert_fusion, f32[1280]{0:T(1024)S(1)} %multiply_subtract_fusion), kind=kOutput, calls=%fused_computation.31 | convolution fusion | flops 2601428736 | bytes 7922224 | tf_op jit(solution)/shard_map/dot_general | solution.py:240
  (123 shorter events, 46.3 us)
Async XLA Ops:
  7.2 142.8 %copy-start = (bf16[256,1024]{1,0:T(8,128)(2,1)S(1)}, bf16[256,1024]{1,0:T(8,128)(2,1)}, u32[]{:S(2)}) copy-start(bf16[256,1024]{1,0:T(8,128)(2,1)} %param.29) | copy-start | bytes 1572868
  7.2 27.5 %all-gather.6.cloned.1.call-start = ((), (), s32[]{:S(2)}) async-start(), calls=%async_computation.1 | async-start | bytes 1310720 | tf_op jit(solution)/shard_map/all_gather | solution.py:128
  11.0 4.1 %copy-start.3 = (bf16[3,1024,128]{2,1,0:T(8,128)(2,1)S(1)}, bf16[3,1024,128]{2,1,0:T(8,128)(2,1)}, u32[]{:S(2)}) copy-start(bf16[3,1024,128]{2,1,0:T(8,128)(2,1)} %param.24) | copy-start | bytes 2359300
  14.9 119.0 %all-reduce.2.cloned.1.call-start = ((), (), s32[]{:S(2)}) async-start(), calls=%async_computation.2 | async-start | bytes 2097152 | tf_op jit(solution)/shard_map/psum | solution.py:188
  34.6 3.2 %copy-start.1 = (bf16[512,1024]{1,0:T(8,128)(2,1)S(1)}, bf16[512,1024]{1,0:T(8,128)(2,1)}, u32[]{:S(2)}) copy-start(bf16[512,1024]{1,0:T(8,128)(2,1)} %all-gather.6.cloned.1.call-done) | copy-start | bytes 3145732
  61.4 18.3 %copy-start.8 = (f32[2]{0:T(128)S(1)}, f32[2]{0:T(128)}, u32[]{:S(2)}) copy-start(f32[2]{0:T(128)} %param.25) | copy-start | bytes 28
  95.3 2.6 copy-start.4
  97.8 79.0 %reduce-scatter.2.cloned.1.call-start = ((), (), s32[]{:S(2)}) async-start(), calls=%async_computation.3 | async-start | bytes 1474560 | tf_op jit(solution)/shard_map/reduce_scatter | solution.py:210
  133.9 12.1 %copy-start.7 = (bf16[2,1024,256]{2,1,0:T(8,128)(2,1)S(1)}, bf16[2,1024,256]{2,1,0:T(8,128)(2,1)}, u32[]{:S(2)}) copy-start(bf16[2,1024,256]{2,1,0:T(8,128)(2,1)} %param.27) | copy-start | bytes 3145732
  135.6 5.1 %collective-permute-start = (bf16[20,1024]{1,0:T(8,128)(2,1)S(1)}, bf16[20,1024]{1,0:T(8,128)(2,1)S(1)}, u32[]{:S(2)}, u32[]{:S(2)}) collective-permute-start(bf16[20,1024]{1,0:T(8,128)(2,1)S(1)} %get-tuple-element.190), channel_id=1, source_target_pairs={{0,4},{4,8},{8,12},{1,5},{5,9},{9,13},{2,6},{6,10},{10,14},{3,7},{... | collective-permute-start | bytes 122888 | tf_op jit(solution)/shard_map/ppermute | solution.py:17
  139.0 6.0 %collective-permute-start.1 = (bf16[20,1024]{1,0:T(8,128)(2,1)S(1)}, bf16[20,1024]{1,0:T(8,128)(2,1)S(1)}, u32[]{:S(2)}, u32[]{:S(2)}) collective-permute-start(bf16[20,1024]{1,0:T(8,128)(2,1)S(1)} %get-tuple-element.191), channel_id=1, source_target_pairs={{4,0},{8,4},{12,8},{5,1},{9,5},{13,9},{6,2},{10,6},{14,10},{7,3},{... | collective-permute-start | bytes 122888 | tf_op jit(solution)/shard_map/ppermute | solution.py:18
  149.9 4.8 %copy-start.5 = (f32[7,512]{1,0:T(8,128)S(1)}, f32[7,512]{1,0:T(8,128)}, u32[]{:S(2)}) copy-start(f32[7,512]{1,0:T(8,128)} %param.31) | copy-start | bytes 43012
  151.5 43.5 %all-gather.8.cloned.1.call-start = ((), (), s32[]{:S(2)}) async-start(), calls=%async_computation.4 | async-start | bytes 1310720 | tf_op jit(solution)/shard_map/all_gather | solution.py:129
  152.0 64.0 %all-gather.10.cloned.1.call-start = ((), (), s32[]{:S(2)}) async-start(), calls=%async_computation.5 | async-start | bytes 1966080 | tf_op jit(solution)/shard_map/all_gather | solution.py:130
  152.6 84.5 %all-gather.12.cloned.1.call-start = ((), (), s32[]{:S(2)}) async-start(), calls=%async_computation.6 | async-start | bytes 1966080 | tf_op jit(solution)/shard_map/all_gather | solution.py:131
  153.2 103.8 %all-gather.14.cloned.1.call-start = ((), (), s32[]{:S(2)}) async-start(), calls=%async_computation.7 | async-start | bytes 1648640 | tf_op jit(solution)/shard_map/all_gather | solution.py:132
  198.3 58.8 %copy-start.6 = (f32[1282]{0:T(1024)S(1)}, f32[1282]{0:T(1024)}, u32[]{:S(2)}) copy-start(f32[1282]{0:T(1024)} %param.35) | copy-start | bytes 15388
  257.0 4.0 %copy-start.2 = (f32[641,1280]{1,0:T(8,128)S(1)}, f32[641,1280]{1,0:T(8,128)}, u32[]{:S(2)}) copy-start(f32[641,1280]{1,0:T(8,128)} %get-tuple-element.253) | copy-start | bytes 9845764
Sparse Core Ops, SparseCore 0:
  15.1 19.5 all-gather.5
  97.9 35.9 all-reduce.1
  151.6 25.1 reduce-scatter.1
  178.2 16.6 all-gather.7
  196.3 19.6 all-gather.9
  217.4 19.6 all-gather.11
  238.6 18.3 all-gather.13
where the time goes:
time: 277 us; the launch traced here: 276 us
  waiting for transfers between devices  135 us (49%)
  other arithmetic  38 us (14%)
  matrix products  37 us (13%)
  blocking collectives  32.1 us (12%)
  between operations  15.2 us (5%)
  local copies, waits for them, and re-layouts  11.3 us (4%)
  starting transfers between devices  5.14 us (2%)
  loops' own time  2.77 us (1%)
    psum x1, waiting for transfers between devices, local(): lax.psum(head_part.astype(jnp.bfloat16), ('head', 'sub'))  36 us
    all_gather x1, waiting for transfers between devices, local(): lax.all_gather(voc_down, ('head', 'sub'), axis=0, tiled=True)  21.1 us
    all_gather x1, waiting for transfers between devices, local(): lax.all_gather(embedded, ('head', 'sub'), axis=1, tiled=True)  18.6 us
    all_gather x1, waiting for transfers between devices, local(): lax.all_gather(voc_up, ('head', 'sub'), axis=0, tiled=True)  17.7 us
    all_gather x1, blocking collectives, local(): value_piece = lax.all_gather(value_rows, 'seq', axis=0, tiled=True)  16.1 us
    all_gather x1, blocking collectives, local(): key_piece = lax.all_gather(key_unit, 'seq', axis=0, tiled=True)  16 us
    all_gather x1, waiting for transfers between devices, local(): lax.all_gather(voc_head, ('head', 'sub'), axis=0, tiled=True)  15.4 us
    select_n x1, other arithmetic, synthesis_tables(): sin_table = jnp.where(edge_bin, 0.0, -factor * jnp.sin(phase_angle))  15.1 us
  transfers between devices with their start and end apart: 9, of which 9 were waited for; matrix products, arithmetic and copies ran while one was open for 11% of the time, Pallas kernels for 0%

commit v1 on v0

--- a/solution.py
+++ b/solution.py
@@ -124,11 +124,41 @@
             matches.astype(jnp.bfloat16), tables[rvq_level], preferred_element_type=jnp.float32
         )
     embedded = embedded.astype(jnp.bfloat16)
+
+    def match_the_streams(join_dim, u_in):
+        view_out = jax.lax.axis_size(("head", "sub"))
+        left_arr, value_now, back = (
+            view_out,
+            jax.lax.axis_index(("head", "sub")),
+            u_in.shape[join_dim],
+        )
+        pieces_in = list(map(lambda pp: (pp, (pp + 1) % left_arr), range(left_arr)))
+        entries = list(map(lambda pp: (pp, (pp - 1) % left_arr), range(left_arr)))
+        x_now = jnp.zeros(
+            (*u_in.shape[:join_dim], left_arr * back, *u_in.shape[join_dim + 1 :]), u_in.dtype
+        )
+        x_now = lax.dynamic_update_slice_in_dim(x_now, u_in, value_now * back, axis=join_dim)
+        upper = val2 = u_in
+        t1 = left_arr // 2
+        t = 1
+        while t < t1 + 1:
+            upper = jax.lax.ppermute(upper, axis_name=("head", "sub"), perm=pieces_in)
+            x_now = lax.dynamic_update_slice_in_dim(
+                x_now, upper, (value_now - t) % left_arr * back, axis=join_dim
+            )
+            if t < left_arr - t1:
+                val2 = jax.lax.ppermute(val2, ("head", "sub"), perm=entries)
+                x_now = lax.dynamic_update_slice_in_dim(
+                    x_now, val2, (value_now + t) % left_arr * back, axis=join_dim
+                )
+            t = t + 1
+        return x_now
+
     inputs, voc_in_full, voc_up_full, voc_down_full, voc_head_full = (
         lax.all_gather(embedded, ("head", "sub"), axis=1, tiled=True),
         lax.all_gather(voc_in, ("head", "sub"), axis=0, tiled=True),
         lax.all_gather(voc_up, ("head", "sub"), axis=0, tiled=True),
-        lax.all_gather(voc_down, ("head", "sub"), axis=0, tiled=True),
+        match_the_streams(0, voc_down),
         lax.all_gather(voc_head, ("head", "sub"), axis=0, tiled=True),
     )
     normed = layer_norm(inputs.astype(jnp.float32)).astype(jnp.bfloat16)

time: 277 us -> 257 us (0.928)
  waiting for transfers between devices: 135 us -> 107 us
  local copies, waits for them, and re-layouts: 11.3 us -> 17.7 us
    all_gather x1 -> x0, waiting for transfers between devices: 21.1 us -> none  [local(): lax.all_gather(voc_down, ('head', 'sub'), axis=0, tiled=True)]
    dynamic_update_slice x0 -> x4, local copies, waits for them, and re-layouts: none -> 5.1 us  [the longest x2 2.52 us: match_the_streams(): lax.dynamic_update_slice_in_dim(x_now, upper, (value_now - t) % left_arr...]
    reduce_scatter x1, waiting for transfers between devices: 4.9 us -> 0.01 us  [local(): lax.psum_scatter(partial_out.astype(jnp.bfloat16), ('head', 'sub'), scatt...]
    all_gather x1, waiting for transfers between devices: 14.1 us -> 9.25 us  [local(): lax.all_gather(voc_in, ('head', 'sub'), axis=0, tiled=True)]
    ppermute x0 -> x3, waiting for transfers between devices: none -> 4.6 us  [the longest x2 4.59 us: match_the_streams(): upper = jax.lax.ppermute(upper, axis_name=('head', 'sub'), perm=pieces_in)]
  transfers between devices with their start and end apart: 9 -> 11, of which waited for: 9 -> 8; matrix products, arithmetic and copies ran while one was open for 11% -> 14% of each run, Pallas kernels for 0% -> 0%
where the time goes in v1:
time: 257 us; the launch traced here: 256 us
  waiting for transfers between devices  107 us (42%)
  other arithmetic  38.5 us (15%)
  matrix products  35.8 us (14%)
  blocking collectives  32.3 us (13%)
  local copies, waits for them, and re-layouts  17.7 us (7%)
  between operations  15.3 us (6%)
  starting transfers between devices  6.77 us (3%)
  loops' own time  2.76 us (1%)
    psum x1, waiting for transfers between devices, local(): lax.psum(head_part.astype(jnp.bfloat16), ('head', 'sub'))  36 us
    all_gather x1, waiting for transfers between devices, local(): lax.all_gather(embedded, ('head', 'sub'), axis=1, tiled=True)  18.6 us
    all_gather x1, waiting for transfers between devices, local(): lax.all_gather(voc_up, ('head', 'sub'), axis=0, tiled=True)  17.7 us
    all_gather x1, blocking collectives, local(): value_piece = lax.all_gather(value_rows, 'seq', axis=0, tiled=True)  16.3 us
    all_gather x1, blocking collectives, local(): key_piece = lax.all_gather(key_unit, 'seq', axis=0, tiled=True)  16 us
    all_gather x1, waiting for transfers between devices, local(): lax.all_gather(voc_head, ('head', 'sub'), axis=0, tiled=True)  15.3 us
    select_n x1, other arithmetic, synthesis_tables(): sin_table = jnp.where(edge_bin, 0.0, -factor * jnp.sin(phase_angle))  15.1 us
    all_gather x1, waiting for transfers between devices, local(): lax.all_gather(voc_in, ('head', 'sub'), axis=0, tiled=True)  9.25 us
  transfers between devices with their start and end apart: 11, of which 8 were waited for; matrix products, arithmetic and copies ran while one was open for 14% of the time, Pallas kernels for 0%

profile of v1, /device:TPU:0, one launch (start us, length us, event | category | flops | bytes accessed | tf_op | source)
XLA Modules:
  0.0 256.3 jit_solution(11266642847124642442)
XLA Ops:
  14.0 18.6 %all-gather.5.cloned.1.call-done = bf16[512,1024]{1,0:T(8,128)(2,1)} async-done(((bf16[512,256]{1,0:T(8,128)(2,1)}), bf16[512,1024]{1,0:T(8,128)(2,1)}) %all-gather.5.cloned.1.call-update) | async-done | bytes 1048592 | tf_op jit(solution)/shard_map/all_gather | solution.py:158
  36.1 2.0 convolution_convert_fusion.2
  38.7 16.0 %all_gather.20 = bf16[2048,128]{0,1:T(8,128)(2,1)S(1)} all-gather(bf16[512,128]{0,1:T(8,128)(2,1)S(1)} %bitcast.157), channel_id=1, replica_groups=mesh['groups'=2,'seq'=4,'head'=2,'sub'=2] {'seq'}, dimensions={0}, use_global_device_ids=true | all-gather | bytes 655360 | tf_op jit(solution)/shard_map/all_gather | solution.py:181
  55.9 1.9 copy.28
  57.8 2.1 multiply_reduce_fusion.5
  59.9 16.3 %all_gather.19 = bf16[2048,128]{1,0:T(8,128)(2,1)S(1)} all-gather(bf16[512,128]{1,0:T(8,128)(2,1)} %convolution_convert_fusion.2), channel_id=1, replica_groups=mesh['groups'=2,'seq'=4,'head'=2,'sub'=2] {'seq'}, dimensions={0}, use_global_device_ids=true | all-gather | bytes 655360 | tf_op jit(solution)/shard_map/all_gather | solution.py:182
  79.0 15.8 %while.15 = (s32[]{:T(128)}, f32[512,2,64]{0,2,1:T(8,128)S(1)}, f32[512,2]{0,1:T(2,128)S(1)}, bf16[4,512,2,64]{1,3,2,0:T(8,128)(2,1)S(1)}, s32[4]{0:T(128)S(1)},...) while((s32[]{:T(128)}, f32[512,2,64]{0,2,1:T(8,128)S(1)}, ...), condition=%wide.region_6.7_spmd.clone, body=%wide.region_4.6_spmd.clone.sunk | while | flops 136972288 | bytes 3032748 | solution.py:208
  94.9 2.4 convolution_convert_fusion.1
  97.4 36.0 %all-reduce.2.cloned.1.call-done = bf16[512,1024]{1,0:T(8,128)(2,1)} async-done(((bf16[512,1024]{1,0:T(8,128)(2,1)}), bf16[512,1024]{1,0:T(8,128)(2,1)}) %all-reduce.2.cloned.1.call-update) | async-done | bytes 1048592 | tf_op jit(solution)/shard_map/psum | solution.py:218
  135.2 3.4 %collective-permute-start = (bf16[20,1024]{1,0:T(8,128)(2,1)S(1)}, bf16[20,1024]{1,0:T(8,128)(2,1)S(1)}, u32[]{:S(2)}, u32[]{:S(2)}) collective-permute-start(bf16[20,1024]{1,0:T(8,128)(2,1)S(1)} %get-tuple-element.190), channel_id=1, source_target_pairs={{0,4},{4,8},{8,12},{1,5},{5,9},{9,13},{2,6},{6,10},{10,14},{3,7},{... | collective-permute-start | bytes 122888 | tf_op jit(solution)/shard_map/ppermute | solution.py:17
  140.3 4.3 %collective-permute-done.1 = bf16[20,1024]{1,0:T(8,128)(2,1)S(1)} collective-permute-done((bf16[20,1024]{1,0:T(8,128)(2,1)S(1)}, bf16[20,1024]{1,0:T(8,128)(2,1)S(1)}, u32[]{:S(2)}, u32[]{:S(2)}) %collective-permute-start.1) | collective-permute-done | bytes 40992 | tf_op jit(solution)/shard_map/ppermute | solution.py:18
  147.1 2.3 multiply_convert_fusion.2
  152.3 1.7 collective-permute-start.3
  154.2 15.1 %multiply_select_fusion = (f32[641,1280]{1,0:T(8,128)}, f32[641,1280]{1,0:T(8,128)}) fusion(f32[641]{0:T(1024)S(1)} %fusion.133, pred[641]{0:T(1024)(128)(4,1)S(1)} %fusion.132, f32[641]{0:T(1024)S(1)} %select_multiply_fusion), kind=kLoop, calls=%fused_computation.20 | loop fusion | flops 9845760 | bytes 6569609 | tf_op jit(solution)/shard_map/jit(_where)/select_n | solution.py:86
  173.2 1.8 constant_dynamic-update-slice_fusion.1
  175.0 4.6 %collective-permute-done.4 = bf16[384,512]{1,0:T(8,128)(2,1)} collective-permute-done((bf16[384,512]{1,0:T(8,128)(2,1)S(1)}, bf16[384,512]{1,0:T(8,128)(2,1)}, u32[]{:S(2)}, u32[]{:S(2)}) %collective-permute-start.4) | collective-permute-done | bytes 393248 | tf_op jit(solution)/shard_map/ppermute | solution.py:145
  179.6 1.8 constant_dynamic-update-slice_fusion
  181.3 1.8 fusion.166
  187.2 9.3 %all-gather.7.cloned.1.call-done = bf16[1024,512]{1,0:T(8,128)(2,1)} async-done(((bf16[256,512]{1,0:T(8,128)(2,1)}), bf16[1024,512]{1,0:T(8,128)(2,1)}) %all-gather.7.cloned.1.call-update) | async-done | bytes 1048592 | tf_op jit(solution)/shard_map/all_gather | solution.py:159
  199.8 17.7 %all-gather.9.cloned.1.call-done = bf16[512,1536]{1,0:T(8,128)(2,1)} async-done(((bf16[128,1536]{1,0:T(8,128)(2,1)}), bf16[512,1536]{1,0:T(8,128)(2,1)}) %all-gather.9.cloned.1.call-update) | async-done | bytes 1572880 | tf_op jit(solution)/shard_map/all_gather | solution.py:160
  217.6 4.3 %fusion.178 = (f32[132]{0:T(256)S(1)}, f32[132,512]{1,0:T(8,128)S(1)}) fusion(bf16[1536,512]{1,0:T(8,128)(2,1)} %constant_dynamic-update-slice_fusion, bf16[512,1536]{1,0:T(8,128)(2,1)} %all-gather.9.cloned.1.call-done, f32[132,512]{1,0:T(8,128)S(1)} %get-tuple-element.185, f32[132]{0:T(256)S(1)} %add_rsqrt_fusion.5, f32[132]{0:T(256)S(1)} %broadcast_multiply_fusion.4, ...), kind=kOutput, calls=%fused_computation.264 | convolution fusion | flops 428752768 | bytes 3958320 | tf_op jit(solution)/shard_map/dot_general | solution.py:259
  222.1 15.3 %all-gather.11.cloned.1.call-done = bf16[512,1282]{0,1:T(8,128)(2,1)} async-done(((bf16[128,1282]{0,1:T(8,128)(2,1)}), bf16[512,1282]{0,1:T(8,128)(2,1)}) %all-gather.11.cloned.1.call-update) | async-done | bytes 1312784 | tf_op jit(solution)/shard_map/all_gather | solution.py:162
  237.4 2.1 convolution_add_fusion
  241.2 6.2 %fusion.19 = f32[132,1280]{1,0:T(8,128)S(1)} fusion(f32[641,1280]{1,0:T(8,128)S(1)} %copy-done.2, f32[641,1280]{1,0:T(8,128)} %get-tuple-element.254, f32[132,641]{1,0:T(8,128)S(1)} %get-tuple-element.199, f32[132,641]{1,0:T(8,128)S(1)} %get-tuple-element.198, f32[132]{0:T(256)S(1)} %and_convert_fusion, f32[1280]{0:T(1024)S(1)} %multiply_subtract_fusion), kind=kOutput, calls=%fused_computation.31 | convolution fusion | flops 2601428736 | bytes 7922224 | tf_op jit(solution)/shard_map/dot_general | solution.py:270
  (135 shorter events, 51.2 us)
Async XLA Ops:
  7.2 142.3 %copy-start = (bf16[256,1024]{1,0:T(8,128)(2,1)S(1)}, bf16[256,1024]{1,0:T(8,128)(2,1)}, u32[]{:S(2)}) copy-start(bf16[256,1024]{1,0:T(8,128)(2,1)} %param.29) | copy-start | bytes 1572868
  7.2 25.4 %all-gather.5.cloned.1.call-start = ((), (), s32[]{:S(2)}) async-start(), calls=%async_computation.1 | async-start | bytes 1310720 | tf_op jit(solution)/shard_map/all_gather | solution.py:158
  7.2 3.8 %copy-start.8 = (bf16[3,1024,256]{2,1,0:T(8,128)(2,1)S(1)}, bf16[3,1024,256]{2,1,0:T(8,128)(2,1)}, u32[]{:S(2)}) copy-start(bf16[3,1024,256]{2,1,0:T(8,128)(2,1)} %param.22) | copy-start | bytes 4718596
  11.0 1.9 copy-start.4
  12.9 120.6 %all-reduce.2.cloned.1.call-start = ((), (), s32[]{:S(2)}) async-start(), calls=%async_computation.2 | async-start | bytes 2097152 | tf_op jit(solution)/shard_map/psum | solution.py:218
  32.6 3.2 %copy-start.1 = (bf16[512,1024]{1,0:T(8,128)(2,1)S(1)}, bf16[512,1024]{1,0:T(8,128)(2,1)}, u32[]{:S(2)}) copy-start(bf16[512,1024]{1,0:T(8,128)(2,1)} %all-gather.5.cloned.1.call-done) | copy-start | bytes 3145732
  59.9 19.1 %copy-start.10 = (f32[2]{0:T(128)S(1)}, f32[2]{0:T(128)}, u32[]{:S(2)}) copy-start(f32[2]{0:T(128)} %param.25) | copy-start | bytes 28
  94.8 2.6 copy-start.5
  97.3 85.8 %reduce-scatter.2.cloned.1.call-start = ((), (), s32[]{:S(2)}) async-start(), calls=%async_computation.3 | async-start | bytes 1474560 | tf_op jit(solution)/shard_map/reduce_scatter | solution.py:240
  133.5 12.1 %copy-start.9 = (bf16[2,1024,256]{2,1,0:T(8,128)(2,1)S(1)}, bf16[2,1024,256]{2,1,0:T(8,128)(2,1)}, u32[]{:S(2)}) copy-start(bf16[2,1024,256]{2,1,0:T(8,128)(2,1)} %param.27) | copy-start | bytes 3145732
  135.2 5.1 %collective-permute-start = (bf16[20,1024]{1,0:T(8,128)(2,1)S(1)}, bf16[20,1024]{1,0:T(8,128)(2,1)S(1)}, u32[]{:S(2)}, u32[]{:S(2)}) collective-permute-start(bf16[20,1024]{1,0:T(8,128)(2,1)S(1)} %get-tuple-element.190), channel_id=1, source_target_pairs={{0,4},{4,8},{8,12},{1,5},{5,9},{9,13},{2,6},{6,10},{10,14},{3,7},{... | collective-permute-start | bytes 122888 | tf_op jit(solution)/shard_map/ppermute | solution.py:17
  138.6 6.0 %collective-permute-start.1 = (bf16[20,1024]{1,0:T(8,128)(2,1)S(1)}, bf16[20,1024]{1,0:T(8,128)(2,1)S(1)}, u32[]{:S(2)}, u32[]{:S(2)}) collective-permute-start(bf16[20,1024]{1,0:T(8,128)(2,1)S(1)} %get-tuple-element.191), channel_id=1, source_target_pairs={{4,0},{8,4},{12,8},{5,1},{9,5},{13,9},{6,2},{10,6},{14,10},{7,3},{... | collective-permute-start | bytes 122888 | tf_op jit(solution)/shard_map/ppermute | solution.py:18
  149.5 2.8 %copy-start.3 = (bf16[384,512]{1,0:T(8,128)(2,1)S(1)}, bf16[384,512]{1,0:T(8,128)(2,1)}, u32[]{:S(2)}) copy-start(bf16[384,512]{1,0:T(8,128)(2,1)} %param.33) | copy-start | bytes 1179652
  149.5 4.7 %copy-start.6 = (f32[7,512]{1,0:T(8,128)S(1)}, f32[7,512]{1,0:T(8,128)}, u32[]{:S(2)}) copy-start(f32[7,512]{1,0:T(8,128)} %param.31) | copy-start | bytes 43012
  151.0 45.5 %all-gather.7.cloned.1.call-start = ((), (), s32[]{:S(2)}) async-start(), calls=%async_computation.4 | async-start | bytes 1310720 | tf_op jit(solution)/shard_map/all_gather | solution.py:159
  151.6 66.0 %all-gather.9.cloned.1.call-start = ((), (), s32[]{:S(2)}) async-start(), calls=%async_computation.5 | async-start | bytes 1966080 | tf_op jit(solution)/shard_map/all_gather | solution.py:160
  152.2 85.2 %all-gather.11.cloned.1.call-start = ((), (), s32[]{:S(2)}) async-start(), calls=%async_computation.6 | async-start | bytes 1648640 | tf_op jit(solution)/shard_map/all_gather | solution.py:162
  152.3 18.0 %collective-permute-start.2 = (bf16[384,512]{1,0:T(8,128)(2,1)S(1)}, bf16[384,512]{1,0:T(8,128)(2,1)S(1)}, u32[]{:S(2)}, u32[]{:S(2)}) collective-permute-start(bf16[384,512]{1,0:T(8,128)(2,1)S(1)} %copy-done.3), channel_id=1, source_target_pairs={{0,1},{1,2},{2,3},{3,0},{4,5},{5,6},{6,7},{7,4},{8,9},{9,10},{10,1... | collective-permute-start | bytes 1179656 | tf_op jit(solution)/shard_map/ppermute | solution.py:145
  152.3 20.9 %collective-permute-start.3 = (bf16[384,512]{1,0:T(8,128)(2,1)S(1)}, bf16[384,512]{1,0:T(8,128)(2,1)}, u32[]{:S(2)}, u32[]{:S(2)}) collective-permute-start(bf16[384,512]{1,0:T(8,128)(2,1)S(1)} %copy-done.3), channel_id=1, source_target_pairs={{0,3},{1,0},{2,1},{3,2},{4,7},{5,4},{6,5},{7,6},{8,11},{9,8},{10,9... | collective-permute-start | bytes 1179656 | tf_op jit(solution)/shard_map/ppermute | solution.py:150
  170.2 9.3 %collective-permute-start.4 = (bf16[384,512]{1,0:T(8,128)(2,1)S(1)}, bf16[384,512]{1,0:T(8,128)(2,1)}, u32[]{:S(2)}, u32[]{:S(2)}) collective-permute-start(bf16[384,512]{1,0:T(8,128)(2,1)S(1)} %collective-permute-done.2), channel_id=1, source_target_pairs={{0,1},{1,2},{2,3},{3,0},{4,5},{5,6},{6,7},{7,4},{8,9},{9,10},{10,1... | collective-permute-start | bytes 1179656 | tf_op jit(solution)/shard_map/ppermute | solution.py:145
  199.8 37.6 %copy-start.7 = (f32[1282]{0:T(1024)S(1)}, f32[1282]{0:T(1024)}, u32[]{:S(2)}) copy-start(f32[1282]{0:T(1024)} %param.35) | copy-start | bytes 15388
  237.4 3.8 %copy-start.2 = (f32[641,1280]{1,0:T(8,128)S(1)}, f32[641,1280]{1,0:T(8,128)}, u32[]{:S(2)}) copy-start(f32[641,1280]{1,0:T(8,128)} %get-tuple-element.253) | copy-start | bytes 9845764
Sparse Core Ops, SparseCore 0:
  13.0 19.5 all-gather.4
  97.4 35.9 all-reduce.1
  151.2 26.2 reduce-scatter.1
  178.9 17.5 all-gather.6
  197.9 19.6 all-gather.8
  219.0 18.3 all-gather.10
